TPU v7x, 128 devices: a whole 4x4x4 slice. The times are simulated.
128 devices in a mesh: seq: 32 (over y, x, z_lo), tp: 4 (over z_hi, core).
Axes of the slice: x: 4, y: 4, z: 4 (z_hi: 2, z_lo: 2; z = z_hi * 2 + z_lo), core: 2. Of those that a mesh axis runs over, the one named last changes fastest.
Arguments:
- hidden_in: bfloat16 [24576, 4096], P(('seq', 'tp')), may hold values from -26 to 26
- norm_gain: float32 [4096], replicated, may hold values from 0.1 to 1.9
- w_qkv: bfloat16 [3, 4096, 2048], P(None, None, 'tp'), may hold values from -1 to 1
- w_out: bfloat16 [2048, 4096], P('tp'), may hold values from -0.125 to 0.125
Outputs:
- datastore: bfloat16 [24576, 4096], P(('seq', 'tp'))
All inputs are finite; a program needn't handle non-finite values.
Results may differ from a plain program's by a relative error of at most 0.006.
Values may be sent and summed in bfloat16 or wider, within the bound.
A program may use at most 128 MiB of HBM per device.

v0:
```python
import jax
import jax.numpy as jnp
from jax import lax
from jax.sharding import PartitionSpec as P

HD = 64
SPAN = 512


epsilon = 1e-06


def extended(block, sides, width):
    for axis, dim in sides:
        count = lax.axis_size(axis)
        forward = [(i, i + 1) for i in range(count - 1)]
        backward = [(target, source) for source, target in forward]
        low = lax.ppermute(
            lax.slice_in_dim(block, block.shape[dim] - width, None, axis=dim), axis, forward
        )
        high = lax.ppermute(lax.slice_in_dim(block, 0, width, axis=dim), axis, backward)
        block = jnp.concatenate([low, block, high], axis=dim)
    return block


def rms_scale(rows_in, norm_gain):
    widened = rows_in.astype(jnp.float32)
    mean_square = jnp.mean(widened * widened, axis=1, keepdims=True)
    return (widened * lax.rsqrt(mean_square + epsilon) * norm_gain[None, :]).astype(jnp.bfloat16)


def attend(queries, keys_pad, values_pad, at_start, at_end):
    span_len = SPAN
    half_len = span_len // 2
    quarter = span_len // 4
    query_rows = queries.shape[0]
    block_count = query_rows // half_len
    head_count = queries.shape[1] // HD
    query_blocks = queries.reshape(block_count, half_len, head_count, HD)
    key_blocks = jnp.stack(
        [
            keys_pad[number * half_len : number * half_len + span_len]
            for number in range(block_count)
        ]
    )
    value_blocks = jnp.stack(
        [
            values_pad[number * half_len : number * half_len + span_len]
            for number in range(block_count)
        ]
    )
    key_blocks = key_blocks.reshape(block_count, span_len, head_count, HD)
    value_blocks = value_blocks.reshape(block_count, span_len, head_count, HD)
    scores = jnp.einsum(
        "bqhd,bkhd->bhqk", query_blocks, key_blocks, preferred_element_type=jnp.float32
    )
    key_place = (
        jnp.arange(block_count, dtype=jnp.int32)[:, None] * half_len
        + jnp.arange(span_len, dtype=jnp.int32)[None, :]
    )
    left_out = jnp.logical_and(at_start, key_place < quarter)
    right_out = jnp.logical_and(at_end, key_place >= query_rows + quarter)
    key_valid = jnp.logical_not(jnp.logical_or(left_out, right_out))
    scores = jnp.where(key_valid[:, None, None, :], scores, -1e30)
    row_max = jnp.max(scores, axis=-1, keepdims=True)
    powers = jnp.exp(scores - row_max)
    weights = (powers / jnp.sum(powers, axis=-1, keepdims=True)).astype(jnp.bfloat16)
    context = jnp.einsum(
        "bhqk,bkhd->bqhd", weights, value_blocks, preferred_element_type=jnp.float32
    )
    return context.astype(jnp.bfloat16).reshape(query_rows, head_count * HD)


def on_device(hidden_in, norm_gain, w_qkv, w_out):
    seq_count = lax.axis_size("seq")
    seq_index = lax.axis_index("seq")
    own_rows = hidden_in.shape[0]
    model_width = hidden_in.shape[1]
    inner_width = w_qkv.shape[2]
    quarter = SPAN // 4
    at_start = seq_index == 0
    at_end = seq_index == seq_count - 1
    normed = lax.all_gather(rms_scale(hidden_in, norm_gain), "tp", axis=0, tiled=True)
    queries = jnp.dot(normed, w_qkv[0], preferred_element_type=jnp.float32).astype(jnp.bfloat16)
    keys_own = jnp.dot(normed, w_qkv[1], preferred_element_type=jnp.float32).astype(jnp.bfloat16)
    values_own = jnp.dot(normed, w_qkv[2], preferred_element_type=jnp.float32).astype(jnp.bfloat16)
    joined = jnp.concatenate([keys_own, values_own], axis=1)
    padded = extended(joined, (("seq", 0),), quarter)
    keys_pad = padded[:, :inner_width]
    values_pad = padded[:, inner_width:]
    context = attend(queries, keys_pad, values_pad, at_start, at_end)
    own_sum = lax.psum_scatter(
        jnp.dot(context, w_out, preferred_element_type=jnp.float32).astype(jnp.bfloat16),
        "tp",
        scatter_dimension=0,
        tiled=True,
    ).astype(jnp.float32)
    new_state = (hidden_in.astype(jnp.float32) + own_sum).astype(jnp.bfloat16)
    stripe_len = own_rows // seq_count
    pieces = new_state.reshape(seq_count, stripe_len, model_width)
    received = lax.all_to_all(pieces, "seq", split_axis=0, concat_axis=0, tiled=True)
    return received.reshape(own_rows, model_width)


def solution(mesh):
    return jax.shard_map(
        on_device,
        mesh=mesh,
        in_specs=(P(("seq", "tp"), None), P(), P(None, None, "tp"), P("tp", None)),
        out_specs=P(("seq", "tp"), None),
        check_vma=False,
    )
```

profile of v0, /device:TPU:1, one launch (start us, length us, event | category | flops | bytes accessed | tf_op | source)
XLA Modules:
  0.0 248.3 jit_solution(113620848852326442)
XLA Ops:
  6.5 0.0 all-gather.2.cloned.1.call-start
  6.5 1.8 fusion.16
  8.3 3.0 %fusion.18 = bf16[192,4096]{1,0:T(8,128)(2,1)} fusion(bf16[192,4096]{1,0:T(8,128)(2,1)} %param.4, f32[4096]{0:T(1024)} %param.5, f32[192]{0:T(256)S(1)} %add_rsqrt_fusion), kind=kLoop, calls=%fused_computation.23 | loop fusion | flops 3145728 | bytes 3162880 | tf_op jit(solution)/shard_map/convert_element_type | solution.py:29
  11.4 0.0 all-gather.2.cloned.1.call-update
  11.4 0.0 reduce-scatter.2.cloned.1.call-start
  11.5 0.1 fusion.52
  11.6 54.2 %all-gather.2.cloned.1.call-done = bf16[768,4096]{1,0:T(8,128)(2,1)} async-done(((bf16[192,4096]{1,0:T(8,128)(2,1)}), bf16[768,4096]{1,0:T(8,128)(2,1)}) %all-gather.2.cloned.1.call-update) | async-done | bytes 6291472 | tf_op jit(solution)/shard_map/all_gather | solution.py:83
  65.7 7.6 %fusion.35 = bf16[768,512]{0,1:T(8,128)(2,1)S(1)} fusion(bf16[768,4096]{1,0:T(8,128)(2,1)} %all-gather.2.cloned.1.call-done, bf16[3,4096,512]{2,1,0:T(8,128)(2,1)} %param.6), kind=kOutput, calls=%fused_computation.38 | convolution fusion | flops 3221618688 | bytes 11272192 | tf_op jit(solution)/shard_map/dot_general | solution.py:86
  73.3 0.0 copy-done.4
  73.3 5.9 %fusion.32 = bf16[768,512]{0,1:T(8,128)(2,1)S(1)} fusion(bf16[768,4096]{1,0:T(8,128)(2,1)S(1)} %copy-done.4, bf16[3,4096,512]{2,1,0:T(8,128)(2,1)} %param.6), kind=kOutput, calls=%fused_computation.37 | convolution fusion | flops 3221618688 | bytes 11272192 | tf_op jit(solution)/shard_map/dot_general | solution.py:85
  79.2 0.8 pad_maximum_fusion.7
  80.1 2.3 collective-permute-start
  82.4 1.3 collective-permute-start.1
  83.7 6.5 %fusion.38 = bf16[768,512]{1,0:T(8,128)(2,1)} fusion(bf16[768,4096]{1,0:T(8,128)(2,1)S(1)} %copy-done.4, bf16[3,4096,512]{2,1,0:T(8,128)(2,1)} %param.6), kind=kOutput, calls=%fused_computation.39 | convolution fusion | flops 3221618688 | bytes 11272192 | tf_op jit(solution)/shard_map/dot_general | solution.py:84
  90.2 2.4 reshape.69
  92.6 0.0 collective-permute-done
  92.6 0.1 collective-permute-done.1
  92.7 2.2 pad_maximum_fusion.5
  94.9 6.3 %fusion.25 = f32[3,8,256,512]{3,2,1,0:T(8,128)} fusion(bf16[1,512,8,64]{1,3,2,0:T(8,128)(2,1)S(1)} %bitcast.35, bf16[1,512,8,64]{1,3,2,0:T(8,128)(2,1)S(1)} %bitcast.36, bf16[1,512,8,64]{1,3,2,0:T(8,128)(2,1)S(1)} %bitcast.34, bf16[3,256,8,64]{3,2,1,0:T(8,128)(2,1)S(1)} %reshape.69), kind=kOutput, calls=%fused_computation.30 | convolution fusion | flops 404226048 | bytes 14942208 | tf_op jit(solution)/shard_map/bqhd,bkhd->bhqk/dot_general | solution.py:54
  101.2 15.4 %fusion.56 = (f32[3,8,256]{2,1,0:T(8,128)S(1)}, f32[3,8,256,512]{3,2,1,0:T(8,128)}) fusion(f32[3,8,256,512]{3,2,1,0:T(8,128)} %fusion.25, pred[3,512]{1,0:T(4,128)(4,1)S(1)} %fusion.52), kind=kOutput, calls=%fused_computation.62 | output fusion | flops 12583423 | bytes 25191936 | tf_op jit(solution)/shard_map/sub | solution.py:66
  116.6 0.0 copy-done.2
  116.6 0.0 copy-start.5
  116.6 6.0 %fusion.44 = bf16[3,256,8,64]{1,3,2,0:T(8,128)(2,1)S(1)} fusion(f32[3,8,256,512]{3,2,1,0:T(8,128)} %get-tuple-element.16, f32[3,8,256]{2,1,0:T(8,128)S(1)} %get-tuple-element.15, bf16[1,512,8,64]{1,3,2,0:T(8,128)(2,1)S(1)} %bitcast.39, bf16[1,512,8,64]{1,3,2,0:T(8,128)(2,1)S(1)} %bitcast.40, bf16[1,512,8,64]{1,3,2,0:T(8,128)(2,1)S(1)} %bitcast.38), kind=kOutput, calls=%fused_computation.41 | convolution fusion | flops 410910720 | bytes 14966784 | tf_op jit(solution)/shard_map/bhqk,bkhd->bqhd/dot_general | solution.py:68
  122.6 0.7 copy.8
  123.2 0.2 copy.11
  123.4 5.4 %convolution_convert_fusion = bf16[768,4096]{1,0:T(8,128)(2,1)} fusion(bf16[768,512]{0,1:T(8,128)(2,1)S(1)} %bitcast.37, bf16[512,4096]{1,0:T(8,128)(2,1)S(1)} %copy-done.5), kind=kOutput, calls=%fused_computation.5 | convolution fusion | flops 3224371200 | bytes 11272192 | tf_op jit(solution)/shard_map/dot_general | solution.py:93
  128.8 0.0 reduce-scatter.2.cloned.1.call-update
  128.8 68.7 %reduce-scatter.2.cloned.1.call-done = bf16[192,4096]{1,0:T(8,128)(2,1)} async-done(((bf16[768,4096]{1,0:T(8,128)(2,1)}), bf16[192,4096]{1,0:T(8,128)(2,1)}) %reduce-scatter.2.cloned.1.call-update) | async-done | bytes 1572880 | tf_op jit(solution)/shard_map/reduce_scatter | solution.py:92
  197.5 3.1 %fusion.19 = bf16[192,4096]{1,0:T(8,128)(2,1)} fusion(bf16[192,4096]{1,0:T(8,128)(2,1)S(1)} %copy-done, bf16[192,4096]{1,0:T(8,128)(2,1)} %reduce-scatter.2.cloned.1.call-done), kind=kLoop, calls=%fused_computation.24 | loop fusion | flops 3145728 | bytes 4718592 | tf_op jit(solution)/shard_map/convert_element_type | solution.py:98
  200.6 2.4 reshape.67
  203.0 34.8 %all_to_all.5 = bf16[32,6,4096]{2,1,0:T(8,128)(2,1)} all-to-all(bf16[32,6,4096]{2,1,0:T(8,128)(2,1)S(1)} %reshape.67), channel_id=1, replica_groups=mesh['seq'=32,'tp'=4] {'seq'}, dimensions={0} | all-to-all | bytes 3145728 | tf_op jit(solution)/shard_map/all_to_all | solution.py:101
  237.8 3.7 %reshape.68 = bf16[192,4096]{1,0:T(8,128)(2,1)} reshape(bf16[32,6,4096]{2,1,0:T(8,128)(2,1)} %all_to_all.5) | data formatting | bytes 3145728 | tf_op jit(solution)/shard_map/reshape | solution.py:102
  (11 shorter events, 0.0 us)
Async XLA Ops:
  6.5 59.2 %all-gather.2.cloned.1.call-start = ((), (), s32[]{:S(2)}) async-start(), calls=%async_computation.2 | async-start | bytes 7864320 | tf_op jit(solution)/shard_map/all_gather | solution.py:83
  11.4 186.1 %reduce-scatter.2.cloned.1.call-start = ((), (), s32[]{:S(2)}) async-start(), calls=%async_computation.3 | async-start | bytes 7864320 | tf_op jit(solution)/shard_map/reduce_scatter | solution.py:92
  65.7 7.6 %copy-start.4 = (bf16[768,4096]{1,0:T(8,128)(2,1)S(1)}, bf16[768,4096]{1,0:T(8,128)(2,1)}, u32[]{:S(2)}) copy-start(bf16[768,4096]{1,0:T(8,128)(2,1)} %all-gather.2.cloned.1.call-done) | copy-start | bytes 18874372
  80.1 12.5 %collective-permute-start = (bf16[128,1024]{0,1:T(8,128)(2,1)}, bf16[128,1024]{0,1:T(8,128)(2,1)S(1)}, u32[]{:S(2)}, u32[]{:S(2)}) collective-permute-start(bf16[128,1024]{0,1:T(8,128)(2,1)} %get-tuple-element.11), channel_id=1, source_target_pairs={{0,4},{4,8},{8,12},{12,16},{16,20},{20,24},{24,28},{28,32},{32,36}... | collective-permute-start | bytes 786440 | tf_op jit(solution)/shard_map/ppermute | solution.py:18
  82.4 10.3 %collective-permute-start.1 = (bf16[128,1024]{0,1:T(8,128)(2,1)}, bf16[128,1024]{0,1:T(8,128)(2,1)}, u32[]{:S(2)}, u32[]{:S(2)}) collective-permute-start(bf16[128,1024]{0,1:T(8,128)(2,1)} %get-tuple-element.12), channel_id=1, source_target_pairs={{4,0},{8,4},{12,8},{16,12},{20,16},{24,20},{28,24},{32,28},{36,32}... | collective-permute-start | bytes 786440 | tf_op jit(solution)/shard_map/ppermute | solution.py:21
  101.2 15.4 %copy-start.1 = (bf16[512,512]{0,1:T(8,128)(2,1)S(1)}, bf16[512,512]{0,1:T(8,128)(2,1)}, u32[]{:S(2)}) copy-start(bf16[512,512]{0,1:T(8,128)(2,1)} %get-tuple-element.5) | copy-start | bytes 1572868
  101.2 15.4 %copy-start.2 = (bf16[512,512]{0,1:T(8,128)(2,1)S(1)}, bf16[512,512]{0,1:T(8,128)(2,1)}, u32[]{:S(2)}) copy-start(bf16[512,512]{0,1:T(8,128)(2,1)} %get-tuple-element.10) | copy-start | bytes 1572868
  101.2 15.4 %copy-start.3 = (bf16[512,512]{0,1:T(8,128)(2,1)S(1)}, bf16[512,512]{0,1:T(8,128)(2,1)}, u32[]{:S(2)}) copy-start(bf16[512,512]{0,1:T(8,128)(2,1)} %get-tuple-element.14) | copy-start | bytes 1572868
  116.6 6.8 %copy-start.5 = (bf16[512,4096]{1,0:T(8,128)(2,1)S(1)}, bf16[512,4096]{1,0:T(8,128)(2,1)}, u32[]{:S(2)}) copy-start(bf16[512,4096]{1,0:T(8,128)(2,1)} %param.7) | copy-start | bytes 12582916
  128.8 68.7 %copy-start = (bf16[192,4096]{1,0:T(8,128)(2,1)S(1)}, bf16[192,4096]{1,0:T(8,128)(2,1)}, u32[]{:S(2)}) copy-start(bf16[192,4096]{1,0:T(8,128)(2,1)} %param.4) | copy-start | bytes 4718596
Sparse Core Ops, SparseCore 0:
  11.5 54.1 all-gather.1
  128.9 68.5 reduce-scatter.1
where the time goes:
time: 250 us; the launch traced here: 248 us
  waiting for transfers between devices  123 us (49%)
  matrix products  37.6 us (15%)
  blocking collectives  34.8 us (14%)
  other arithmetic  26.4 us (11%)
  between operations  13.5 us (5%)
  local copies, waits for them, and re-layouts  9.4 us (4%)
  starting transfers between devices  3.62 us (1%)
    reduce_scatter x1, waiting for transfers between devices, on_device(): lax.psum_scatter(jnp.dot(context, w_out, preferred_element_type=jnp.float...  68.7 us
    all_gather x1, waiting for transfers between devices, on_device(): lax.all_gather(rms_scale(hidden_in, norm_gain), 'tp', axis=0, tiled=True)  54.2 us
    all_to_all x1, blocking collectives, on_device(): lax.all_to_all(pieces, 'seq', split_axis=0, concat_axis=0, tiled=True)  34.8 us
    sub x1, other arithmetic, attend(): powers = jnp.exp(scores - row_max)  15.4 us
    dot_general x1, matrix products, on_device(): jnp.dot(normed, w_qkv[2], preferred_element_type=jnp.float32)  7.61 us
    dot_general x1, matrix products, on_device(): jnp.dot(normed, w_qkv[0], preferred_element_type=jnp.float32)  6.49 us
    dot_general x1, matrix products, attend(): jnp.einsum('bqhd,bkhd->bhqk', query_blocks, key_blocks, preferred_element...  6.26 us
    dot_general x1, matrix products, attend(): jnp.einsum('bhqk,bkhd->bqhd', weights, value_blocks, preferred_element_ty...  5.96 us
  transfers between devices with their start and end apart: 4, of which 3 were waited for; matrix products, arithmetic and copies ran while one was open for 4% of the time, Pallas kernels for 0%

commit v1 on v0

v1 whole, which is shorter than its diff:
```python
import jax
import jax.numpy as jnp
from jax import lax
from jax.experimental import pallas as pl
from jax.experimental.pallas import tpu as pltpu
from jax.sharding import PartitionSpec as P

D = 4096
HD = 64
OWN = 192
HALF = 384
QUARTER = 128
WIDTH = 512
epsilon = 1e-06
MESH = pl.DeviceIdType.MESH
f32 = jnp.float32
bf16 = jnp.bfloat16


def rows(start, size, unit=8):
    return pl.ds(pl.multiple_of(start, unit), size)


def waiter(ref, sem):
    pltpu.make_async_copy(ref, ref, sem).wait()


def spread_matrix():
    i = lax.broadcasted_iota(jnp.int32, (256, OWN), 0)
    j = lax.broadcasted_iota(jnp.int32, (256, OWN), 1)
    r = i & 7
    return jnp.where((r < 6) & (j == (i >> 3) * 6 + r), 1.0, 0.0).astype(bf16)


def gather_matrix():
    i = lax.broadcasted_iota(jnp.int32, (OWN, 256), 1)
    j = lax.broadcasted_iota(jnp.int32, (OWN, 256), 0)
    r = i & 7
    return jnp.where((r < 6) & (j == (i >> 3) * 6 + r), 1.0, 0.0).astype(bf16)


def kernel(
    hid, gain, wqkv, wout, out,
    H, NB, WQ, WO, QKV, CTX, CS, CR, XS, XR, CD,
    loc, wsem, agS, agR, fwS, fwR, sibS, sibR, wsS, wsR, p1S, p1R, s1S, s1R, s2S, s2R, wfS, wfR, hS, hR, kvS, kvR, cS, cR,
):
    s = lax.axis_index("seq")
    t = lax.axis_index("tp")
    y, x, zl = s // 8, lax.rem(s // 2, 4), lax.rem(s, 2)
    zh, c = t // 2, lax.rem(t, 2)
    zo, sib = 1 - zh, 1 - c
    tsib, topp = zh * 2 + sib, zo * 2 + c
    me = s * 4 + t

    barrier = pltpu.get_barrier_semaphore()

    def greet(i, carry):
        o = lax.rem(me + i, 128)
        pl.semaphore_signal(barrier, 1, device_id=(o // 4, lax.rem(o, 4)), device_id_type=MESH)
        return carry

    own_rows = rows(t * OWN, OWN, 64)
    load_h = pltpu.make_async_copy(hid, H.at[own_rows], loc.at[0])
    load_h.start()
    load_wq = pltpu.make_async_copy(wqkv, WQ, loc.at[1])
    load_wq.start()
    load_wo = pltpu.make_async_copy(wout, WO.at[t], loc.at[2])
    load_wo.start()

    lax.fori_loop(1, 128, greet, 0)
    pl.semaphore_wait(barrier, 127)

    def remote(src, dst, ss, rs, seq, tp):
        return pltpu.make_async_remote_copy(src, dst, ss, rs, device_id=(seq, tp), device_id_type=MESH)

    p0, p1 = y * 4 + x, x * 4 + y
    pmine = jnp.where(c == 0, p0, p1)
    seq_cross = y * 8 + x * 2 + (1 - zl)
    first = []
    for cc in range(2):
        cols = pl.ds(cc * 2048, 2048)
        cp = remote(wout.at[rows(pmine * 32, 32, 32), cols], WO.at[t, rows(pmine * 32, 32, 32), cols],
                    p1S.at[cc], p1R.at[c], seq_cross, zo * 2 + cc)
        cp.start()
        first.append(cp)
    to_sib = remote(hid, H.at[own_rows], sibS, sibR, s, tsib)
    to_sib.start()
    ag = []
    for j in range(3):
        cp = remote(hid.at[pl.ds(j * 64, 64)], H.at[rows(t * OWN + j * 64, 64, 64)], agS.at[j], agR.at[j], s, topp)
        cp.start()
        ag.append(cp)
    w_sib = remote(wout, WO.at[t], wsS, wsR, s, tsib)
    w_sib.start()

    load_h.wait()
    spread = spread_matrix()

    def spread_hidden(n, carry):
        cols = rows(n * 512, 512, 512)
        XS[:, cols] = jnp.dot(spread, H[own_rows, cols], preferred_element_type=f32).astype(bf16)
        return carry

    lax.fori_loop(0, 8, spread_hidden, 0)

    def send_hidden(i, carry):
        o = lax.rem(s + i * 11, 32)
        remote(XS.at[rows(o * 8, 8)], XR.at[rows(s * 8, 8)], hS, hR, o, t).start()
        return carry

    lax.fori_loop(1, 32, send_hidden, 0)
    own_hidden = pltpu.make_async_copy(XS.at[rows(s * 8, 8)], XR.at[rows(s * 8, 8)], loc.at[3])
    own_hidden.start()

    def norm(base):
        def body(i, carry):
            w = H[rows(base + i * 16, 16, 16), :].astype(f32)
            scale = lax.rsqrt(jnp.sum(w * w, axis=1, keepdims=True) * (1.0 / D) + epsilon)
            NB[rows(i * 16, 16, 16), :] = (w * scale * gain[...]).astype(bf16)
            return carry
        lax.fori_loop(0, HALF // 16, body, 0)

    def project(base):
        def body(k, carry):
            QKV[k, rows(QUARTER + base, HALF, 128), :] = jnp.dot(
                NB[...], WQ[k], preferred_element_type=f32).astype(bf16)
            return carry
        lax.fori_loop(0, 3, body, 0)

    sh0, sh1 = zo * 2, zo * 2 + 1
    mycols = rows(c * 2048, 2048, 2048)

    waiter(H.at[own_rows], sibR)
    norm(zh * HALF)
    for cc in range(2):
        waiter(WO.at[0, pl.ds(0, 32), pl.ds(0, 2048)], p1R.at[cc])
    second = []
    for d in range(1, 4):
        xo, yo = lax.rem(x + d, 4), lax.rem(y + d, 4)
        sl = WO.at[sh0, rows(p0 * 32, 32, 32), mycols]
        cp = remote(sl, sl, s1S.at[0], s1R.at[0], y * 8 + xo * 2 + zl, t)
        cp.start()
        sl = WO.at[sh1, rows(p1 * 32, 32, 32), mycols]
        cp = remote(sl, sl, s1S.at[1], s1R.at[1], yo * 8 + x * 2 + zl, t)
        cp.start()
    load_wq.wait()
    project(zh * HALF)
    for k in range(2):
        waiter(WO.at[0, pl.ds(0, 96), pl.ds(0, 2048)], s1R.at[k])
    for d in range(1, 4):
        xo, yo = lax.rem(x + d, 4), lax.rem(y + d, 4)
        sl = WO.at[sh0, rows(y * 128, 128, 128), mycols]
        remote(sl, sl, s2S.at[0], s2R.at[0], yo * 8 + x * 2 + zl, t).start()
        sl = WO.at[sh1, rows(x * 128, 128, 128), mycols]
        remote(sl, sl, s2S.at[1], s2R.at[1], y * 8 + xo * 2 + zl, t).start()

    fw = []
    for j in range(3):
        sl = H.at[rows(topp * OWN + j * 64, 64, 64)]
        waiter(sl, agR.at[j])
        cp = remote(sl, sl, fwS.at[j], fwR.at[j], s, tsib)
        cp.start()
        fw.append(cp)
    for j in range(3):
        waiter(H.at[pl.ds(0, 64)], fwR.at[j])
    norm(zo * HALF)
    project(zo * HALF)

    lo = QKV.at[pl.ds(1, 2), pl.ds(0, 128)]
    hi = QKV.at[pl.ds(1, 2), pl.ds(896, 128)]

    @pl.when(s > 0)
    def _():
        remote(QKV.at[pl.ds(1, 2), pl.ds(128, 128)], hi, kvS.at[0], kvR.at[0], s - 1, t).start()

    @pl.when(s < 31)
    def _():
        remote(QKV.at[pl.ds(1, 2), pl.ds(768, 128)], lo, kvS.at[1], kvR.at[1], s + 1, t).start()

    @pl.when(s == 0)
    def _():
        QKV[pl.ds(1, 2), pl.ds(0, 128), :] = jnp.zeros((2, 128, WIDTH), bf16)

    @pl.when(s == 31)
    def _():
        QKV[pl.ds(1, 2), pl.ds(896, 128), :] = jnp.zeros((2, 128, WIDTH), bf16)

    @pl.when(s > 0)
    def _():
        waiter(lo, kvR.at[1])

    @pl.when(s < 31)
    def _():
        waiter(hi, kvR.at[0])

    lane = lax.broadcasted_iota(jnp.int32, (256, 128), 1)
    place = lax.broadcasted_iota(jnp.int32, (1, 512), 1)

    def attend(i, carry):
        b, pair = i // 4, lax.rem(i, 4)
        cols = rows(pair * 128, 128, 128)
        q = QKV[0, rows(QUARTER + b * 256, 256, 128), cols]
        k = QKV[1, rows(b * 256, 512, 128), cols]
        v = QKV[2, rows(b * 256, 512, 128), cols]
        first_ok = jnp.where((s == 0) & (b == 0), 128, 0)
        last_ok = jnp.where((s == 31) & (b == 2), 384, 512)
        bias = jnp.where((place >= first_ok) & (place < last_ok), 0.0, -1e30)
        parts = []
        for h in range(2):
            qh = jnp.where((lane < HD) == (h == 0), q, jnp.zeros_like(q))
            sc = lax.dot_general(qh, k, (((1,), (1,)), ((), ())), preferred_element_type=f32) + bias
            m = jnp.max(sc, axis=1, keepdims=True)
            p = jnp.exp(sc - m)
            total = jnp.sum(p, axis=1, keepdims=True)
            o = jnp.dot(p.astype(bf16), v, preferred_element_type=f32)
            parts.append(o / total)
        CTX[rows(b * 256, 256, 256), cols] = jnp.where(lane < HD, parts[0], parts[1]).astype(bf16)
        return carry

    lax.fori_loop(0, 12, attend, 0)

    def spread_context(n, carry):
        CS[rows(n * 256, 256, 256), :] = jnp.dot(
            spread, CTX[rows(n * OWN, OWN, 64), :], preferred_element_type=f32).astype(bf16)
        return carry

    lax.fori_loop(0, 4, spread_context, 0)
    ccols = rows(t * WIDTH, WIDTH, 512)

    def send_context(i, carry):
        o = lax.rem(me + i * 37, 128)
        os_, ot = o // 4, lax.rem(o, 4)
        remote(CS.at[rows(ot * 256 + os_ * 8, 8)], CR.at[rows(s * 8, 8), ccols], cS, cR, os_, ot).start()
        return carry

    lax.fori_loop(1, 128, send_context, 0)
    own_context = pltpu.make_async_copy(CS.at[rows(t * 256 + s * 8, 8)], CR.at[rows(s * 8, 8), ccols], loc.at[4])
    own_context.start()

    for k in range(2):
        waiter(WO.at[0, pl.ds(0, 384), pl.ds(0, 2048)], s2R.at[k])
    sl = WO.at[pl.ds(zo * 2, 2), :, mycols]
    w_fw = remote(sl, sl, wfS, wfR, s, tsib)
    w_fw.start()

    pack = gather_matrix()
    load_wo.wait()
    waiter(WO.at[0], wsR)
    waiter(WO.at[pl.ds(0, 2), :, pl.ds(0, 2048)], wfR)
    own_hidden.wait()
    waiter(XR.at[pl.ds(0, 248)], hR)
    own_context.wait()
    waiter(CS.at[pl.ds(0, 1016)], cR)
    CD[...] = jnp.dot(pack, CR[...], preferred_element_type=f32).astype(bf16)

    def finish(n, carry):
        cols = rows(n * 512, 512, 512)
        acc = jnp.dot(pack, XR[:, cols], preferred_element_type=f32)
        prod = jnp.zeros((OWN, 512), f32)
        for k in range(4):
            prod += jnp.dot(CD[:, k * 512:(k + 1) * 512], WO[k, :, cols], preferred_element_type=f32)
        out[:, cols] = (acc + prod).astype(bf16)
        return carry

    lax.fori_loop(0, 8, finish, 0)

    for cp in first:
        cp.wait_send()
    to_sib.wait_send()
    for cp in ag + fw:
        cp.wait_send()
    w_sib.wait_send()
    w_fw.wait_send()
    for k in range(2):
        waiter(WO.at[0, pl.ds(0, 96), pl.ds(0, 2048)], s1S.at[k])
        waiter(WO.at[0, pl.ds(0, 384), pl.ds(0, 2048)], s2S.at[k])
    waiter(XS.at[pl.ds(0, 248)], hS)
    waiter(CS.at[pl.ds(0, 1016)], cS)

    @pl.when(s > 0)
    def _():
        waiter(lo, kvS.at[0])

    @pl.when(s < 31)
    def _():
        waiter(hi, kvS.at[1])


def on_device(hidden_in, norm_gain, w_qkv, w_out):
    dma = pltpu.SemaphoreType.DMA
    return pl.pallas_call(
        kernel,
        out_shape=jax.ShapeDtypeStruct((OWN, D), bf16),
        in_specs=[
            pl.BlockSpec(memory_space=pl.ANY),
            pl.BlockSpec(memory_space=pltpu.VMEM),
            pl.BlockSpec(memory_space=pl.ANY),
            pl.BlockSpec(memory_space=pl.ANY),
        ],
        out_specs=pl.BlockSpec(memory_space=pltpu.VMEM),
        scratch_shapes=[
            pltpu.VMEM((4 * OWN, D), bf16),
            pltpu.VMEM((HALF, D), bf16),
            pltpu.VMEM((3, D, WIDTH), bf16),
            pltpu.VMEM((4, WIDTH, D), bf16),
            pltpu.VMEM((3, 1024, WIDTH), bf16),
            pltpu.VMEM((4 * OWN, WIDTH), bf16),
            pltpu.VMEM((1024, WIDTH), bf16),
            pltpu.VMEM((256, 4 * WIDTH), bf16),
            pltpu.VMEM((256, D), bf16),
            pltpu.VMEM((256, D), bf16),
            pltpu.VMEM((OWN, 4 * WIDTH), bf16),
            dma((5,)), dma(()), dma((3,)), dma((3,)), dma((3,)), dma((3,)),
            dma(()), dma(()), dma(()), dma(()), dma((2,)), dma((2,)),
            dma((2,)), dma((2,)), dma((2,)), dma((2,)), dma(()), dma(()),
            dma(()), dma(()), dma((2,)), dma((2,)), dma(()), dma(()),
        ],
        compiler_params=pltpu.CompilerParams(
            collective_id=0, has_side_effects=True, vmem_limit_bytes=64000 * 1024
        ),
    )(hidden_in, norm_gain.reshape(1, D), w_qkv, w_out)


def solution(mesh):
    return jax.shard_map(
        on_device,
        mesh=mesh,
        in_specs=(P(("seq", "tp"), None), P(), P(None, None, "tp"), P("tp", None)),
        out_specs=P(("seq", "tp"), None),
        check_vma=False,
    )
```

time: 250 us -> 129 us (0.52)
  Pallas kernels: 0 us -> 126 us
  waiting for transfers between devices: 123 us -> 0 us
  matrix products: 37.6 us -> 0 us
  blocking collectives: 34.8 us -> 0 us
  other arithmetic: 26.4 us -> 0 us
  between operations: 13.5 us -> 0.01 us
  local copies, waits for them, and re-layouts: 9.4 us -> 2.7 us
  starting transfers between devices: 3.62 us -> 0 us
    pallas_call x0 -> x1, Pallas kernels: none -> 126 us  [on_device(): pl.pallas_call(kernel, out_shape=jax.ShapeDtypeStruct((OWN, D), bf16), in...]
    reduce_scatter x1 -> x0, waiting for transfers between devices: 68.7 us -> none  [on_device(): lax.psum_scatter(jnp.dot(context, w_out, preferred_element_type=jnp.float...]
    all_gather x1 -> x0, waiting for transfers between devices: 54.2 us -> none  [on_device(): lax.all_gather(rms_scale(hidden_in, norm_gain), 'tp', axis=0, tiled=True)]
    dot_general x6 -> x0, matrix products: 37.6 us -> none  [the longest x1 7.61 us: on_device(): jnp.dot(normed, w_qkv[2], preferred_element_type=jnp.float32)]
    all_to_all x1 -> x0, blocking collectives: 34.8 us -> none  [on_device(): lax.all_to_all(pieces, 'seq', split_axis=0, concat_axis=0, tiled=True)]
    sub x1 -> x0, other arithmetic: 15.4 us -> none  [attend(): powers = jnp.exp(scores - row_max)]
    reshape x3 -> x0, local copies, waits for them, and re-layouts: 8.53 us -> none  [the longest x1 3.66 us: on_device(): return received.reshape(own_rows, model_width)]
    convert_element_type x2 -> x0, other arithmetic: 6.12 us -> none  [the longest x1 3.09 us: on_device(): new_state = (hidden_in.astype(jnp.float32) + own_sum).astype(jnp.bfloat16)]
  transfers between devices with their start and end apart: 4 -> 0, of which waited for: 3 -> 0; matrix products, arithmetic and copies ran while one was open for 4% -> 0% of each run, Pallas kernels for 0% -> 0%
where the time goes in v1:
time: 129 us
  Pallas kernels  126 us (98%)
  local copies, waits for them, and re-layouts  2.7 us (2%)
    pallas_call x1, Pallas kernels, on_device(): pl.pallas_call(kernel, out_shape=jax.ShapeDtypeStruct((OWN, D), bf16), in...  126 us
    unnamed x1, local copies, waits for them, and re-layouts  2.7 us

profile of v1, /device:TPU:1, one launch (start us, length us, event | category | flops | bytes accessed | tf_op | source)
XLA Modules:
  0.0 128.7 jit_solution(14076965290503779223)
XLA Ops:
  0.0 125.9 %shard_map.46 = bf16[192,4096]{1,0:T(8,128)(2,1)} custom-call(bf16[192,4096]{1,0:T(8,128)(2,1)} %hid.1, f32[1,4096]{1,0:T(1,128)} %bitcast.1, bf16[3,4096,512]{2,1,0:T(8,128)(2,1)} %wqkv.1, bf16[512,4096]{1,0:T(8,128)(2,1)} %wout.1), custom_call_target="tpu_custom_call" | custom-call | tf_op jit(solution)/shard_map/pallas_call | solution.py:291
  125.9 2.7 %copy.6 = bf16[192,4096]{1,0:T(8,128)(2,1)} copy(bf16[192,4096]{1,0:T(8,128)(2,1)} %shard_map.46) | data formatting | bytes 3145728
